TPU v7x, 32 devices: a whole 2x2x4 slice. The times are simulated.
32 devices in a mesh: groups: 2 (over x), tm: 4 (over y, core), tile: 4 (over z).
Axes of the slice: x: 2, y: 2, z: 4, core: 2. Of those that a mesh axis runs over, the one named last changes fastest.
Arguments:
- activations: float32 [24, 8, 64, 384], P(('groups', 'tm'), 'tile'), parts along dimension 0, may hold values from -200 to 200, as said below
- gain_attention: float32 [384], replicated, may hold values from 0.1 to 1.9
- w_query: float32 [384, 384], replicated, may hold values from -10 to 10, as said below
- w_key: float32 [384, 384], replicated, may hold values from -10 to 10, as said below
- w_value: float32 [384, 384], replicated, may hold values from -0.3125 to 0.3125
- w_out: float32 [384, 384], replicated, may hold values from -0.3125 to 0.3125
- gain_conv: float32 [384], replicated, may hold values from 0.1 to 1.9
- conv_weight: float32 [27, 384, 384], P(None, 'tm'), may hold values from -0.0625 to 0.0625
Outputs:
- attended: float32 [24, 8, 64, 384], P(('groups', 'tm'), 'tile'), parts along dimension 0
- conv_out: float32 [24, 8, 64, 384], P(('groups', 'tm'), 'tile'), parts along dimension 0
There are 2 independent parts, one for each index of `groups`. A program takes and returns all parts, laid end to end along the dimension named above; an argument that names none is the same for every part. Nothing has to cross between parts.
Inputs may be any that keep to these rules, and one draw needn't show every extreme that they name: `activations`: finite latent features. `w_query`: finite projection entries. `w_key`: finite projection entries.
All inputs are finite; a program needn't handle non-finite values.
Results may differ from a plain program's by a relative error of at most 0.00023.
Values sent between devices are 32-bit elements; how exact they have to be, the bound alone decides.
A program may use at most 128 MiB of HBM per device.

v0:
```python
import math
import jax
import jax.numpy as jnp
from jax import lax
from jax.sharding import PartitionSpec as P


def from_behind(block, axis, distance):
    devices = range(lax.axis_size(axis))
    route = [(i - distance, i) for i in devices if i - distance in devices]
    return lax.ppermute(block, axis, route)


def padded_2(x, sides, width):
    for axis, dim in sides:
        size, length = (lax.axis_size(axis), x.shape[dim])
        up = [(i, (i + 1) % size) for i in range(size - 1)]
        down = [(j, i) for i, j in up]
        last = lax.slice_in_dim(x, length - width, length, axis=dim)
        leading = lax.slice_in_dim(x, 0, width, axis=dim)
        before = lax.ppermute(last, axis, up)
        after = lax.ppermute(leading, axis, down)
        x = jnp.concatenate([before, x, after], axis=dim)
    return x


def rms_scale(values, gain):
    return values * lax.rsqrt(jnp.mean(values * values, axis=-1, keepdims=True) + 1e-06) * gain


def tap_columns(source, frame_count, row_count, width_cells):
    pieces = []
    for shift_t in range(3):
        for shift_y in range(3):
            for shift_x in range(3):
                pieces.append(
                    source[
                        ...,
                        shift_t : shift_t + frame_count,
                        shift_y : shift_y + row_count,
                        shift_x : shift_x + width_cells,
                        :,
                    ]
                )
    joined = jnp.concatenate(pieces, axis=-1)
    return joined.reshape(-1, joined.shape[-1])


def body(activations, gain_attention, w_query, w_key, w_value, w_out, gain_conv, conv_weight):
    highest = lax.Precision.HIGHEST
    frame_count, row_count, width_cells, channels = activations.shape
    tokens = row_count * width_cells
    pixels = frame_count * tokens
    scale = 1.0 / math.sqrt(channels)
    normed = rms_scale(activations, gain_attention).reshape(pixels, channels)
    queries = jnp.dot(normed, w_query, precision=highest).reshape(frame_count, tokens, channels)
    key_rows = jnp.dot(normed, w_key, precision=highest).reshape(frame_count, tokens, channels)
    values = jnp.dot(normed, w_value, precision=highest).reshape(frame_count, tokens, channels)
    running = jnp.full((frame_count, tokens), -1e30, jnp.float32)
    key_piece = lax.all_gather(key_rows, "tile", axis=1, tiled=True)
    value_piece = lax.all_gather(values, "tile", axis=1, tiled=True)
    scores = jnp.einsum("fqc,fkc->fqk", queries, key_piece, precision=highest) * scale
    largest = jnp.maximum(running, jnp.max(scores, axis=-1))
    powers = jnp.exp(scores - largest[..., None])
    summed = jnp.sum(powers, axis=-1)
    accumulated = jnp.einsum("fqk,fkc->fqc", powers, value_piece, precision=highest)
    running, summed, accumulated = (largest, summed, accumulated)
    mixed = accumulated / summed[..., None]
    attended = activations + jnp.dot(
        mixed.reshape(pixels, channels), w_out, precision=highest
    ).reshape(activations.shape)
    hidden = jax.nn.silu(rms_scale(attended, gain_conv))
    cached = from_behind(hidden[frame_count - 2 :], "tm", 1)
    stacked = jnp.concatenate([cached, hidden], axis=0)
    padded = padded_2(stacked, (("tile", 1),), 1)
    padded = jnp.pad(padded, ((0, 0), (0, 0), (1, 1), (0, 0)))
    piece = lax.all_gather(conv_weight, "tm", axis=1, tiled=True)
    count = piece.shape[1]
    columns = tap_columns(padded, frame_count, row_count, width_cells)
    conv_out = jnp.dot(columns, piece.reshape(27 * count, channels), precision=highest)
    return (attended, conv_out.reshape(activations.shape))


def solution(mesh):
    return jax.shard_map(
        body,
        mesh=mesh,
        in_specs=(
            P(("groups", "tm"), "tile", None, None),
            P(),
            P(),
            P(),
            P(),
            P(),
            P(),
            P(None, "tm", None),
        ),
        out_specs=(
            P(("groups", "tm"), "tile", None, None),
            P(("groups", "tm"), "tile", None, None),
        ),
        check_vma=False,
    )
```

profile of v0, /device:TPU:0, one launch (start us, length us, event | category | flops | bytes accessed | tf_op | source)
XLA Modules:
  0.0 256.4 jit_solution(7575440983940319005)
XLA Ops:
  7.2 1.3 multiply_reduce_fusion.1
  8.5 1.2 multiply_multiply_fusion
  9.7 3.1 %fusion.8 = f32[3,128,384]{2,1,0:T(8,128)} fusion(f32[3,128,384]{2,1,0:T(8,128)S(1)} %bitcast.33, f32[384,384]{1,0:T(8,128)} %param.11), kind=kOutput, calls=%fused_computation.50 | convolution fusion | flops 679477248 | bytes 1769472 | tf_op jit(solution)/shard_map/dot_general | solution.py:57
  13.0 3.1 %fusion.6 = f32[3,128,384]{2,1,0:T(8,128)} fusion(f32[3,128,384]{2,1,0:T(8,128)S(1)} %bitcast.34, f32[384,384]{1,0:T(8,128)} %param.12), kind=kOutput, calls=%fused_computation.48 | convolution fusion | flops 679477248 | bytes 1769472 | tf_op jit(solution)/shard_map/dot_general | solution.py:58
  16.2 0.7 all-gather.8.cloned.1.call-update
  16.9 2.3 fusion.10
  19.2 47.0 %all-gather.4.cloned.1.call-done = f32[3,512,384]{2,1,0:T(8,128)} async-done(((f32[3,128,384]{2,1,0:T(8,128)}), f32[3,512,384]{2,1,0:T(8,128)}) %all-gather.4.cloned.1.call-update) | async-done | bytes 2359312 | tf_op jit(solution)/shard_map/all_gather | solution.py:60
  66.2 4.3 %fusion.15 = (f32[3,128]{1,0:T(4,128)S(1)}, f32[3,128,512]{2,1,0:T(8,128)S(1)}) fusion(f32[3,128,384]{2,1,0:T(8,128)S(1)} %fusion.10, f32[3,512,384]{2,1,0:T(8,128)} %all-gather.4.cloned.1.call-done), kind=kOutput, calls=%fused_computation.65 | convolution fusion | flops 906362496 | bytes 3737088 | tf_op jit(solution)/shard_map/fqc,fkc->fqk/dot_general | solution.py:62
  70.5 0.3 fusion.1
  70.8 46.9 %all-gather.6.cloned.1.call-done = f32[3,512,384]{2,1,0:T(8,128)} async-done(((f32[3,128,384]{2,1,0:T(8,128)}), f32[3,512,384]{2,1,0:T(8,128)}) %all-gather.6.cloned.1.call-update) | async-done | bytes 2359312 | tf_op jit(solution)/shard_map/all_gather | solution.py:61
  117.7 3.5 %convolution_divide_fusion = f32[3,128,384]{2,1,0:T(8,128)S(1)} fusion(f32[3,512,384]{2,1,0:T(8,128)} %all-gather.6.cloned.1.call-done, f32[3,128,512]{2,1,0:T(8,128)S(1)} %get-tuple-element.7, f32[3,128]{1,0:T(4,128)S(1)} %broadcast_maximum_fusion, f32[3,128]{1,0:T(4,128)S(1)} %fusion.1), kind=kOutput, calls=%fused_computation.16 | convolution fusion | flops 906313728 | bytes 3738624 | tf_op jit(solution)/shard_map/fqk,fkc->fqc/dot_general | solution.py:66
  121.2 1.4 multiply_reduce_fusion
  122.9 1.8 collective-permute-start
  124.7 1.3 collective-permute-done
  126.1 1.6 collective-permute-start.1
  127.7 1.5 collective-permute-start.2
  129.2 4.8 %collective-permute-done.1 = f32[5,1,64,384]{3,2,1,0:T(8,128)S(1)} collective-permute-done((f32[5,1,64,384]{3,2,1,0:T(8,128)S(1)}, f32[5,1,64,384]{3,2,1,0:T(8,128)S(1)}, u32[]{:S(2)}, u32[]{:S(2)}) %collective-permute-start.1) | collective-permute-done | bytes 491552 | tf_op jit(solution)/shard_map/ppermute | solution.py:21
  134.0 4.5 %collective-permute-done.2 = f32[5,1,64,384]{3,2,1,0:T(8,128)S(1)} collective-permute-done((f32[5,1,64,384]{3,2,1,0:T(8,128)S(1)}, f32[5,1,64,384]{3,2,1,0:T(8,128)S(1)}, u32[]{:S(2)}, u32[]{:S(2)}) %collective-permute-start.2) | collective-permute-done | bytes 491552 | tf_op jit(solution)/shard_map/ppermute | solution.py:22
  138.5 0.4 pad_maximum_fusion
  139.2 0.9 slice_dynamic-update-slice_fusion.23
  140.0 0.9 slice_dynamic-update-slice_fusion.22
  141.0 0.9 slice_dynamic-update-slice_fusion.21
  141.9 0.9 slice_dynamic-update-slice_fusion.20
  142.8 0.9 fusion.3
  143.7 1.0 slice_dynamic-update-slice_fusion.19
  144.7 0.9 slice_dynamic-update-slice_fusion.18
  145.6 0.9 slice_dynamic-update-slice_fusion.17
  146.5 0.9 slice_dynamic-update-slice_fusion.16
  147.4 0.9 slice_dynamic-update-slice_fusion.15
  148.3 0.9 slice_dynamic-update-slice_fusion.14
  149.2 0.9 slice_dynamic-update-slice_fusion.13
  150.1 0.9 slice_dynamic-update-slice_fusion.12
  151.0 0.9 fusion.4
  151.9 0.9 slice_dynamic-update-slice_fusion.11
  152.9 0.9 slice_dynamic-update-slice_fusion.10
  153.8 0.9 slice_dynamic-update-slice_fusion.9
  154.7 0.9 slice_dynamic-update-slice_fusion.8
  155.6 0.9 slice_dynamic-update-slice_fusion.7
  156.5 0.9 slice_dynamic-update-slice_fusion.6
  157.4 0.9 slice_dynamic-update-slice_fusion.5
  158.4 0.9 slice_dynamic-update-slice_fusion.4
  159.2 1.1 constant_dynamic-update-slice_fusion
  160.4 0.9 slice_dynamic-update-slice_fusion.3
  161.3 1.0 slice_dynamic-update-slice_fusion.2
  162.3 0.9 slice_dynamic-update-slice_fusion.1
  163.1 0.9 slice_dynamic-update-slice_fusion
  164.0 55.2 %all-gather.8.cloned.1.call-done = f32[27,384,384]{2,1,0:T(8,128)} async-done(((f32[27,96,384]{2,1,0:T(8,128)}), f32[27,384,384]{2,1,0:T(8,128)}) %all-gather.8.cloned.1.call-update) | async-done | bytes 15925264 | tf_op jit(solution)/shard_map/all_gather | solution.py:77
  219.2 30.7 %fusion.16 = f32[3,2,64,384]{3,2,1,0:T(8,128)} fusion(f32[3,2,64,10368]{3,2,1,0:T(8,128)} %slice_dynamic-update-slice_fusion, f32[10368,384,1,1]{1,0,3,2:T(8,128)} %bitcast.32), kind=kOutput, calls=%fused_computation.66 | convolution fusion | flops 18345885696 | bytes 32440320 | tf_op jit(solution)/shard_map/dot_general | solution.py:80
  (20 shorter events, 0.8 us)
Async XLA Ops:
  7.2 114.0 %copy-start = (f32[384,384]{1,0:T(8,128)S(1)}, f32[384,384]{1,0:T(8,128)}, u32[]{:S(2)}) copy-start(f32[384,384]{1,0:T(8,128)} %param.13) | copy-start | bytes 1769476
  7.2 114.0 %copy-start.1 = (f32[3,2,64,384]{3,2,1,0:T(8,128)S(1)}, f32[3,2,64,384]{3,2,1,0:T(8,128)}, u32[]{:S(2)}) copy-start(f32[3,2,64,384]{3,2,1,0:T(8,128)} %param.8) | copy-start | bytes 1769476
  7.2 115.5 %copy-start.3 = (f32[384]{0:T(512)S(1)}, f32[384]{0:T(512)}, u32[]{:S(2)}) copy-start(f32[384]{0:T(512)} %param.14) | copy-start | bytes 4612
  7.2 59.0 %all-gather.4.cloned.1.call-start = ((), (), s32[]{:S(2)}) async-start(), calls=%async_computation | async-start | bytes 2949120 | tf_op jit(solution)/shard_map/all_gather | solution.py:60
  12.9 104.8 %all-gather.6.cloned.1.call-start = ((), (), s32[]{:S(2)}) async-start(), calls=%async_computation.1 | async-start | bytes 2949120 | tf_op jit(solution)/shard_map/all_gather | solution.py:61
  16.1 203.1 %all-gather.8.cloned.1.call-start = ((), (), s32[]{:S(2)}) async-start(), calls=%async_computation.2 | async-start | bytes 19906560 | tf_op jit(solution)/shard_map/all_gather | solution.py:77
  122.6 36.6 %copy-start.2 = (f32[3,2,64,384]{3,2,1,0:T(8,128)}, f32[3,2,64,384]{3,2,1,0:T(8,128)S(1)}, u32[]{:S(2)}) copy-start(f32[3,2,64,384]{3,2,1,0:T(8,128)S(1)} %get-tuple-element.9) | copy-start | bytes 1769476
  122.9 3.1 %collective-permute-start = (f32[2,2,64,384]{3,2,1,0:T(8,128)S(1)}, f32[2,2,64,384]{3,2,1,0:T(8,128)S(1)}, u32[]{:S(2)}, u32[]{:S(2)}) collective-permute-start(f32[2,2,64,384]{3,2,1,0:T(8,128)S(1)} %slice.135), channel_id=1, source_target_pairs={{0,4},{4,8},{8,12},{1,5},{5,9},{9,13},{2,6},{6,10},{10,14},{3,7},{... | collective-permute-start | bytes 1179656 | tf_op jit(solution)/shard_map/ppermute | solution.py:11
  126.1 8.0 %collective-permute-start.1 = (f32[5,1,64,384]{3,2,1,0:T(8,128)S(1)}, f32[5,1,64,384]{3,2,1,0:T(8,128)S(1)}, u32[]{:S(2)}, u32[]{:S(2)}) collective-permute-start(f32[5,1,64,384]{3,2,1,0:T(8,128)S(1)} %get-tuple-element.4), channel_id=1, source_target_pairs={{0,1},{1,2},{2,3},{4,5},{5,6},{6,7},{8,9},{9,10},{10,11},{12,13},{... | collective-permute-start | bytes 1474568 | tf_op jit(solution)/shard_map/ppermute | solution.py:21
  127.7 10.8 %collective-permute-start.2 = (f32[5,1,64,384]{3,2,1,0:T(8,128)S(1)}, f32[5,1,64,384]{3,2,1,0:T(8,128)S(1)}, u32[]{:S(2)}, u32[]{:S(2)}) collective-permute-start(f32[5,1,64,384]{3,2,1,0:T(8,128)S(1)} %get-tuple-element.5), channel_id=1, source_target_pairs={{1,0},{2,1},{3,2},{5,4},{6,5},{7,6},{9,8},{10,9},{11,10},{13,12},{... | collective-permute-start | bytes 1474568 | tf_op jit(solution)/shard_map/ppermute | solution.py:22
Sparse Core Ops, SparseCore 0:
  13.0 53.1 all-gather.3
  68.3 49.2 all-gather.5
  119.2 99.9 all-gather.7
where the time goes:
time: 257 us; the launch traced here: 256 us
  waiting for transfers between devices  160 us (62%)
  matrix products  48.5 us (19%)
  local copies, waits for them, and re-layouts  22 us (9%)
  between operations  13.9 us (5%)
  other arithmetic  6.63 us (3%)
  starting transfers between devices  5 us (2%)
    all_gather x1, waiting for transfers between devices, body(): piece = lax.all_gather(conv_weight, 'tm', axis=1, tiled=True)  55.2 us
    all_gather x1, waiting for transfers between devices, body(): key_piece = lax.all_gather(key_rows, 'tile', axis=1, tiled=True)  47 us
    all_gather x1, waiting for transfers between devices, body(): value_piece = lax.all_gather(values, 'tile', axis=1, tiled=True)  46.9 us
    dot_general x1, matrix products, body(): jnp.dot(columns, piece.reshape(27 * count, channels), precision=highest)  30.7 us
    unnamed x31, local copies, waits for them, and re-layouts  21 us
  transfers between devices with their start and end apart: 6, of which 6 were waited for; matrix products, arithmetic and copies ran while one was open for 16% of the time, Pallas kernels for 0%

commit v1 on v0

--- a/solution.py
+++ b/solution.py
@@ -57,8 +57,11 @@
     key_rows = jnp.dot(normed, w_key, precision=highest).reshape(frame_count, tokens, channels)
     values = jnp.dot(normed, w_value, precision=highest).reshape(frame_count, tokens, channels)
     running = jnp.full((frame_count, tokens), -1e30, jnp.float32)
-    key_piece = lax.all_gather(key_rows, "tile", axis=1, tiled=True)
-    value_piece = lax.all_gather(values, "tile", axis=1, tiled=True)
+    key_piece, value_piece = jnp.split(
+        lax.all_gather(jnp.concatenate([key_rows, values], axis=0), "tile", axis=1, tiled=True),
+        [key_rows.shape[0]],
+        axis=0,
+    )
     scores = jnp.einsum("fqc,fkc->fqk", queries, key_piece, precision=highest) * scale
     largest = jnp.maximum(running, jnp.max(scores, axis=-1))
     powers = jnp.exp(scores - largest[..., None])

time: 257 us -> 249 us (0.969)
  waiting for transfers between devices: 160 us -> 151 us
    all_gather x2 -> x1, waiting for transfers between devices: 93.9 us -> 89.2 us  [body(): lax.all_gather(jnp.concatenate([key_rows, values], axis=0), 'tile', axis=...]
    all_gather x1, waiting for transfers between devices: 55.2 us -> 50.5 us  [body(): piece = lax.all_gather(conv_weight, 'tm', axis=1, tiled=True)]
  transfers between devices with their start and end apart: 6 -> 5, of which waited for: 6 -> 5; matrix products, arithmetic and copies ran while one was open for 16% -> 15% of each run, Pallas kernels for 0% -> 0%
where the time goes in v1:
time: 249 us; the launch traced here: 247 us
  waiting for transfers between devices  151 us (61%)
  matrix products  47.1 us (19%)
  local copies, waits for them, and re-layouts  22 us (9%)
  between operations  14.2 us (6%)
  other arithmetic  7.6 us (3%)
  starting transfers between devices  4.51 us (2%)
    all_gather x1, waiting for transfers between devices, body(): lax.all_gather(jnp.concatenate([key_rows, values], axis=0), 'tile', axis=...  89.2 us
    all_gather x1, waiting for transfers between devices, body(): piece = lax.all_gather(conv_weight, 'tm', axis=1, tiled=True)  50.5 us
    dot_general x1, matrix products, body(): jnp.dot(columns, piece.reshape(27 * count, channels), precision=highest)  30.7 us
    unnamed x31, local copies, waits for them, and re-layouts  21.1 us
  transfers between devices with their start and end apart: 5, of which 5 were waited for; matrix products, arithmetic and copies ran while one was open for 15% of the time, Pallas kernels for 0%

profile of v1, /device:TPU:0, one launch (start us, length us, event | category | flops | bytes accessed | tf_op | source)
XLA Modules:
  0.0 246.5 jit_solution(5883097428468144847)
XLA Ops:
  7.2 1.3 multiply_reduce_fusion.1
  8.5 1.2 multiply_multiply_fusion
  9.7 2.3 fusion.16
  12.1 2.3 fusion.18
  14.4 1.1 pad_maximum_fusion.1
  15.6 0.7 all-gather.5.cloned.1.call-update
  16.3 2.3 fusion.20
  18.6 89.2 %all-gather.3.cloned.1.call-done = f32[6,512,384]{2,1,0:T(8,128)} async-done(((f32[6,128,384]{2,1,0:T(8,128)}), f32[6,512,384]{2,1,0:T(8,128)}) %all-gather.3.cloned.1.call-update) | async-done | bytes 4718608 | tf_op jit(solution)/shard_map/all_gather | solution.py:61
  107.8 4.3 %fusion.25 = (f32[3,128]{1,0:T(4,128)S(1)}, f32[3,128,512]{2,1,0:T(8,128)S(1)}) fusion(f32[3,128,384]{2,1,0:T(8,128)S(1)} %fusion.20, f32[6,512,384]{2,1,0:T(8,128)} %all-gather.3.cloned.1.call-done), kind=kOutput, calls=%fused_computation.70 | convolution fusion | flops 906362496 | bytes 3737088 | tf_op jit(solution)/shard_map/fqc,fkc->fqk/dot_general | solution.py:65
  112.1 0.3 fusion.11
  112.4 3.7 %fusion.8 = f32[3,128,384]{2,1,0:T(8,128)S(1)} fusion(f32[6,512,384]{2,1,0:T(8,128)} %all-gather.3.cloned.1.call-done, f32[3,128,512]{2,1,0:T(8,128)S(1)} %get-tuple-element.7, f32[3,128]{1,0:T(4,128)S(1)} %broadcast_maximum_fusion, f32[3,128]{1,0:T(4,128)S(1)} %fusion.11), kind=kOutput, calls=%fused_computation.20 | convolution fusion | flops 906313728 | bytes 3738624 | tf_op jit(solution)/shard_map/fqk,fkc->fqc/dot_general | solution.py:69
  116.1 1.4 multiply_reduce_fusion
  117.9 1.6 collective-permute-start
  119.5 1.4 collective-permute-done
  121.0 1.3 collective-permute-start.1
  122.3 1.5 collective-permute-start.2
  123.8 4.8 %collective-permute-done.1 = f32[5,1,64,384]{3,2,1,0:T(8,128)S(1)} collective-permute-done((f32[5,1,64,384]{3,2,1,0:T(8,128)S(1)}, f32[5,1,64,384]{3,2,1,0:T(8,128)S(1)}, u32[]{:S(2)}, u32[]{:S(2)}) %collective-permute-start.1) | collective-permute-done | bytes 491552 | tf_op jit(solution)/shard_map/ppermute | solution.py:21
  128.6 4.4 %collective-permute-done.2 = f32[5,1,64,384]{3,2,1,0:T(8,128)S(1)} collective-permute-done((f32[5,1,64,384]{3,2,1,0:T(8,128)S(1)}, f32[5,1,64,384]{3,2,1,0:T(8,128)S(1)}, u32[]{:S(2)}, u32[]{:S(2)}) %collective-permute-start.2) | collective-permute-done | bytes 491552 | tf_op jit(solution)/shard_map/ppermute | solution.py:22
  133.0 0.3 pad_maximum_fusion
  133.6 0.9 slice_dynamic-update-slice_fusion.23
  134.5 1.0 slice_dynamic-update-slice_fusion.22
  135.5 0.9 slice_dynamic-update-slice_fusion.21
  136.4 0.9 slice_dynamic-update-slice_fusion.20
  137.3 0.9 fusion.13
  138.2 0.9 slice_dynamic-update-slice_fusion.19
  139.1 0.9 slice_dynamic-update-slice_fusion.18
  140.0 0.9 slice_dynamic-update-slice_fusion.17
  140.9 0.9 slice_dynamic-update-slice_fusion.16
  141.8 1.0 slice_dynamic-update-slice_fusion.15
  142.8 0.9 slice_dynamic-update-slice_fusion.14
  143.7 0.9 slice_dynamic-update-slice_fusion.13
  144.6 0.9 slice_dynamic-update-slice_fusion.12
  145.5 0.9 fusion.14
  146.4 0.9 slice_dynamic-update-slice_fusion.11
  147.3 0.9 slice_dynamic-update-slice_fusion.10
  148.2 0.9 slice_dynamic-update-slice_fusion.9
  149.1 0.9 slice_dynamic-update-slice_fusion.8
  150.0 0.9 slice_dynamic-update-slice_fusion.7
  150.9 0.9 slice_dynamic-update-slice_fusion.6
  151.8 0.9 slice_dynamic-update-slice_fusion.5
  152.7 0.9 slice_dynamic-update-slice_fusion.4
  153.7 1.1 constant_dynamic-update-slice_fusion
  154.8 0.9 slice_dynamic-update-slice_fusion.3
  155.7 0.9 slice_dynamic-update-slice_fusion.2
  156.6 0.9 slice_dynamic-update-slice_fusion.1
  157.5 0.9 slice_dynamic-update-slice_fusion
  158.5 50.5 %all-gather.5.cloned.1.call-done = f32[27,384,384]{2,1,0:T(8,128)} async-done(((f32[27,96,384]{2,1,0:T(8,128)}), f32[27,384,384]{2,1,0:T(8,128)}) %all-gather.5.cloned.1.call-update) | async-done | bytes 15925264 | tf_op jit(solution)/shard_map/all_gather | solution.py:80
  209.0 30.7 %fusion.26 = f32[3,2,64,384]{3,2,1,0:T(8,128)} fusion(f32[3,2,64,10368]{3,2,1,0:T(8,128)} %slice_dynamic-update-slice_fusion, f32[10368,384,1,1]{1,0,3,2:T(8,128)} %bitcast.30), kind=kOutput, calls=%fused_computation.71 | convolution fusion | flops 18345885696 | bytes 32440320 | tf_op jit(solution)/shard_map/dot_general | solution.py:83
  (18 shorter events, 0.7 us)
Async XLA Ops:
  7.2 108.9 %copy-start = (f32[384,384]{1,0:T(8,128)S(1)}, f32[384,384]{1,0:T(8,128)}, u32[]{:S(2)}) copy-start(f32[384,384]{1,0:T(8,128)} %param.13) | copy-start | bytes 1769476
  7.2 108.9 %copy-start.1 = (f32[3,2,64,384]{3,2,1,0:T(8,128)S(1)}, f32[3,2,64,384]{3,2,1,0:T(8,128)}, u32[]{:S(2)}) copy-start(f32[3,2,64,384]{3,2,1,0:T(8,128)} %param.8) | copy-start | bytes 1769476
  7.2 110.4 %copy-start.3 = (f32[384]{0:T(512)S(1)}, f32[384]{0:T(512)}, u32[]{:S(2)}) copy-start(f32[384]{0:T(512)} %param.14) | copy-start | bytes 4612
  7.2 100.6 %all-gather.3.cloned.1.call-start = ((), (), s32[]{:S(2)}) async-start(), calls=%async_computation | async-start | bytes 5898240 | tf_op jit(solution)/shard_map/all_gather | solution.py:61
  15.5 193.5 %all-gather.5.cloned.1.call-start = ((), (), s32[]{:S(2)}) async-start(), calls=%async_computation.1 | async-start | bytes 19906560 | tf_op jit(solution)/shard_map/all_gather | solution.py:80
  117.5 36.1 %copy-start.2 = (f32[3,2,64,384]{3,2,1,0:T(8,128)}, f32[3,2,64,384]{3,2,1,0:T(8,128)S(1)}, u32[]{:S(2)}) copy-start(f32[3,2,64,384]{3,2,1,0:T(8,128)S(1)} %get-tuple-element.9) | copy-start | bytes 1769476
  117.9 3.0 %collective-permute-start = (f32[2,2,64,384]{3,2,1,0:T(8,128)S(1)}, f32[2,2,64,384]{3,2,1,0:T(8,128)S(1)}, u32[]{:S(2)}, u32[]{:S(2)}) collective-permute-start(f32[2,2,64,384]{3,2,1,0:T(8,128)S(1)} %slice.135), channel_id=1, source_target_pairs={{0,4},{4,8},{8,12},{1,5},{5,9},{9,13},{2,6},{6,10},{10,14},{3,7},{... | collective-permute-start | bytes 1179656 | tf_op jit(solution)/shard_map/ppermute | solution.py:11
  121.0 7.6 %collective-permute-start.1 = (f32[5,1,64,384]{3,2,1,0:T(8,128)S(1)}, f32[5,1,64,384]{3,2,1,0:T(8,128)S(1)}, u32[]{:S(2)}, u32[]{:S(2)}) collective-permute-start(f32[5,1,64,384]{3,2,1,0:T(8,128)S(1)} %get-tuple-element.4), channel_id=1, source_target_pairs={{0,1},{1,2},{2,3},{4,5},{5,6},{6,7},{8,9},{9,10},{10,11},{12,13},{... | collective-permute-start | bytes 1474568 | tf_op jit(solution)/shard_map/ppermute | solution.py:21
  122.3 10.7 %collective-permute-start.2 = (f32[5,1,64,384]{3,2,1,0:T(8,128)S(1)}, f32[5,1,64,384]{3,2,1,0:T(8,128)S(1)}, u32[]{:S(2)}, u32[]{:S(2)}) collective-permute-start(f32[5,1,64,384]{3,2,1,0:T(8,128)S(1)} %get-tuple-element.5), channel_id=1, source_target_pairs={{1,0},{2,1},{3,2},{5,4},{6,5},{7,6},{9,8},{10,9},{11,10},{13,12},{... | collective-permute-start | bytes 1474568 | tf_op jit(solution)/shard_map/ppermute | solution.py:22
Sparse Core Ops, SparseCore 0:
  15.7 92.0 all-gather.2
  109.4 99.5 all-gather.4
